TPU v7x, 32 devices: a whole 2x2x4 slice. The times are simulated.
32 devices in a mesh: sub: 16 (over z, y, core), coarse: 2 (over x).
Axes of the slice: x: 2, y: 2, z: 4, core: 2. Of those that a mesh axis runs over, the one named last changes fastest.
Arguments:
- loads: float32 [32, 32, 32, 128], P(('sub', 'coarse')), may hold values from -6 to 6
- diag_blocks: float32 [32, 32, 128, 128], P(('sub', 'coarse')), may hold values from -0.2 to 6.2
- off_blocks: float32 [32, 32, 2, 128, 128], P(('sub', 'coarse')), may hold values from -0.25 to 0.25
- off_index: int32 [32, 32, 2], P(('sub', 'coarse')), may hold values from 0 to 31, as said below
- couple_blocks: float32 [32, 2, 128, 128], P(('sub', 'coarse')), may hold values from -0.5 to 0.5
- basis: float32 [32, 128, 32, 128], P(('sub', 'coarse')), may hold values from -0.09375 to 0.09375
- coarse_blocks: float32 [32, 6, 128, 128], P(('sub', 'coarse')), may hold values from -0.21875 to 0.21875
- coarse_index: int32 [32, 6], P(('sub', 'coarse')), may hold values from 0 to 31, as said below
Outputs:
- solution: float32 [32, 32, 32, 128], P(('sub', 'coarse'))
- residual: float32 [32, 32, 32, 128], P(('sub', 'coarse'))
Inputs may be any that keep to these rules, and one draw needn't show every extreme that they name: `off_index`: the 2 entries of a block row name different blocks of the same subdomain, none of them the row's own block. `coarse_index`: the 6 entries of a row name different subdomains, the first being the row's own subdomain g and the second g - 1 counted round.
All inputs are finite; a program needn't handle non-finite values.
Results may differ from a plain program's by a relative error of at most 0.0001.
Values sent between devices are 32-bit elements; how exact they have to be, the bound alone decides.
A program may use at most 128 MiB of HBM per device.

v0:
```python
import jax
import jax.numpy as jnp
from jax import lax
from jax.sharding import PartitionSpec as P

ORDER = 5
ITERS = 2


highest = lax.Precision.HIGHEST
theta_mid = 5.0
delta_half = 4.0


def padded_2(block, sides, width):
    for axis, dim in sides:
        count = lax.axis_size(axis)
        forward = [(i, i + 1) for i in range(count - 1)]
        backward = [(target, source) for source, target in forward]
        low = lax.ppermute(
            lax.slice_in_dim(block, block.shape[dim] - width, None, axis=dim), axis, forward
        )
        high = lax.ppermute(lax.slice_in_dim(block, 0, width, axis=dim), axis, backward)
        block = jnp.concatenate([low, block, high], axis=dim)
    return block


def own_rows(own, left_block, right_block, diag, offs, index, couple):
    result = jnp.einsum("cbk,bik->cbi", own, diag, precision=highest)
    picked = jnp.take(own, index, axis=1)
    result = result + jnp.einsum("cbjk,bjik->cbi", picked, offs, precision=highest)
    first = result[:, 0] + jnp.einsum("ck,ik->ci", left_block, couple[0], precision=highest)
    last = result[:, -1] + jnp.einsum("ck,ik->ci", right_block, couple[1], precision=highest)
    return result.at[:, 0].set(first).at[:, -1].set(last)


def padded_rows(padded, diag, offs, index, couple, left_diag, left_up, right_diag, right_low):
    middle = own_rows(padded[:, 1:-1], padded[:, 0], padded[:, -1], diag, offs, index, couple)
    top = jnp.einsum("ck,ik->ci", padded[:, 0], left_diag, precision=highest)
    top = top + jnp.einsum("ck,ik->ci", padded[:, 1], left_up, precision=highest)
    bottom = jnp.einsum("ck,ik->ci", padded[:, -1], right_diag, precision=highest)
    bottom = bottom + jnp.einsum("ck,ik->ci", padded[:, -2], right_low, precision=highest)
    return jnp.concatenate([top[:, None], middle, bottom[:, None]], axis=1)


def chebyshev(padded, diag, offs, index, couple, left_diag, left_up, right_diag, right_low):
    sigma = theta_mid / delta_half
    rho_now = 1.0 / sigma
    direction = padded / theta_mid
    smooth = jnp.zeros_like(padded)
    for step in range(ORDER):
        smooth = smooth + direction
        if step + 1 < ORDER:
            misfit = padded - padded_rows(
                smooth, diag, offs, index, couple, left_diag, left_up, right_diag, right_low
            )
            rho_next = 1.0 / (2.0 * sigma - rho_now)
            direction = rho_next * rho_now * direction + 2.0 * rho_next / delta_half * misfit
            rho_now = rho_next
    return smooth


def coarse_term(piece, columns, blocks):
    count = piece.shape[0]
    pick = (columns[:, None] == jnp.arange(count, dtype=jnp.int32)[None, :]).astype(jnp.float32)
    chosen = jnp.einsum("jp,pck->jck", pick, piece, precision=highest)
    return jnp.einsum("jck,jik->ci", chosen, blocks, precision=highest)


def per_device(
    loads, diag_blocks, off_blocks, off_index, couple_blocks, basis, coarse_blocks, coarse_index
):
    diag = diag_blocks[0]
    offs = off_blocks[0]
    index = off_index[0]
    couple = couple_blocks[0]
    vectors = basis[0]
    blocks = coarse_blocks[0]
    columns = coarse_index[0]
    rim_pack = jnp.stack([jnp.stack([diag[0], couple[0]]), jnp.stack([diag[-1], couple[1]])])
    beside = padded_2(rim_pack, (("sub", 0),), 1)
    left_diag, left_up = (beside[0, 0], beside[0, 1])
    right_diag, right_low = (beside[3, 0], beside[3, 1])
    resid = loads[0]
    solution = jnp.zeros_like(resid)
    for step in range(ITERS):
        padded = padded_2(resid, (("sub", 1),), 1)
        coeffs = jnp.einsum("cbi,kbi->ck", resid, vectors, precision=highest)
        width = lax.axis_size("coarse")
        across = lax.all_gather(coeffs[None], "coarse", axis=0, tiled=True)
        piece = lax.all_gather(across[None], "sub", axis=0, tiled=True)
        flat = piece.reshape((piece.shape[0] * width,) + piece.shape[2:])
        coarse_sol = coarse_term(flat, columns, blocks)
        smooth = chebyshev(
            padded, diag, offs, index, couple, left_diag, left_up, right_diag, right_low
        )
        edge = smooth[:, 1:-1] + jnp.einsum("ck,kbi->cbi", coarse_sol, vectors, precision=highest)
        rims = jnp.stack([smooth[:, 0], smooth[:, -1]], axis=1)
        arrived = padded_2(rims, (("sub", 1),), 1)
        first = edge[:, 0] + arrived[:, 0]
        last = edge[:, -1] + arrived[:, 3]
        change = edge.at[:, 0].set(first).at[:, -1].set(last)
        padded_change = padded_2(change, (("sub", 1),), 1)
        left_block, right_block = (padded_change[:, 0], padded_change[:, -1])
        solution = solution + change
        resid = resid - own_rows(change, left_block, right_block, diag, offs, index, couple)
    return (solution[None], resid[None])


def solution(mesh):
    in_specs = (
        P(("sub", "coarse"), None, None, None),
        P(("sub", "coarse"), None, None, None),
        P(("sub", "coarse"), None, None, None, None),
        P(("sub", "coarse"), None, None),
        P(("sub", "coarse"), None, None, None),
        P(("sub", "coarse"), None, None, None),
        P(("sub", "coarse"), None, None, None),
        P(("sub", "coarse"), None),
    )
    out_specs = (P(("sub", "coarse"), None, None, None), P(("sub", "coarse"), None, None, None))
    return jax.shard_map(
        per_device, mesh=mesh, in_specs=in_specs, out_specs=out_specs, check_vma=False
    )
```

profile of v0, /device:TPU:1, one launch (start us, length us, event | category | flops | bytes accessed | tf_op | source)
XLA Modules:
  0.0 286.8 jit_solution(16975925575847320079)
XLA Ops:
  5.1 4.6 %collective-permute-start.2 = (f32[1,2,128,128]{3,2,1,0:T(8,128)}, f32[1,2,128,128]{3,2,1,0:T(8,128)S(1)}, u32[]{:S(2)}, u32[]{:S(2)}) collective-permute-start(f32[1,2,128,128]{3,2,1,0:T(8,128)} %maximum_bitcast_fusion), channel_id=1, source_target_pairs={{0,2},{2,4},{4,6},{6,8},{8,10},{10,12},{12,14},{14,16},{16,18},{18... | collective-permute-start | bytes 393224 | tf_op jit(solution)/shard_map/ppermute | solution.py:20
  18.8 3.4 %all-gather = f32[64,128]{1,0:T(8,128)S(1)} all-gather(f32[32,128]{1,0:T(8,128)S(1)} %fusion.192), channel_id=2, replica_groups=mesh['sub'=16,'coarse'=2] {'coarse'}, dimensions={0}, use_global_device_ids=true | all-gather | bytes 49152 | tf_op jit(solution)/shard_map/all_gather | solution.py:90
  22.2 24.8 %all-gather.1 = f32[32,32,128]{2,1,0:T(8,128)S(1)} all-gather(f32[2,32,128]{2,1,0:T(8,128)S(1)} %bitcast.684), channel_id=3, replica_groups=mesh['sub'=16,'coarse'=2] {'sub'}, dimensions={0}, use_global_device_ids=true | all-gather | bytes 557056 | tf_op jit(solution)/shard_map/all_gather | solution.py:91
  51.4 7.0 %fusion.66 = f32[32,32,128]{2,1,0:T(8,128)S(1)} fusion(f32[1,32,2,128,128]{4,3,2,1,0:T(8,128)} %param.60, f32[32,2,32,128]{3,2,1,0:T(8,128)} %bitcast.675, pred[32,2]{1,0:T(8,128)(4,1)S(1)} %copy.65), kind=kOutput, calls=%fused_computation.64 | convolution fusion | flops 402915328 | bytes 5767232 | tf_op jit(solution)/shard_map/cbjk,bjik->cbi/dot_general | solution.py:31
  58.4 3.4 %fusion.99 = f32[32,32,128]{2,0,1:T(8,128)S(1)} fusion(f32[32,32,128]{2,1,0:T(8,128)S(1)} %fusion.66, f32[1,32,128,128]{3,2,1,0:T(8,128)S(1)} %copy-done.8, f32[32,1,128]{2,0,1:T(8,128)S(1)} %copy-done.53, f32[32,32,128]{2,0,1:T(8,128)S(1)} %bitcast.668, f32[32,1,128]{2,0,1:T(8,128)S(1)} %copy-done.48), kind=kOutput, calls=%fused_computation.75 | convolution fusion | flops 201875456 | bytes 3702784 | tf_op jit(solution)/shard_map/cbk,bik->cbi/dot_general | solution.py:29
  72.5 7.0 %fusion.69 = f32[32,32,128]{2,1,0:T(8,128)S(1)} fusion(f32[1,32,2,128,128]{4,3,2,1,0:T(8,128)} %param.60, f32[32,2,32,128]{3,2,1,0:T(8,128)} %bitcast.676, pred[32,2]{1,0:T(8,128)(4,1)S(1)} %copy.65), kind=kOutput, calls=%fused_computation.65 | convolution fusion | flops 402915328 | bytes 5767232 | tf_op jit(solution)/shard_map/cbjk,bjik->cbi/dot_general | solution.py:31
  79.6 3.9 %fusion.105 = f32[32,32,128]{2,0,1:T(8,128)S(1)} fusion(f32[32,32,128]{2,1,0:T(8,128)S(1)} %fusion.69, f32[32,34,128]{2,0,1:T(8,128)S(1)} %copy-done.33, f32[1,32,128,128]{3,2,1,0:T(8,128)S(1)} %copy-done.9), kind=kOutput, calls=%fused_computation.77 | convolution fusion | flops 201457664 | bytes 3702784 | tf_op jit(solution)/shard_map/cbk,bik->cbi/dot_general | solution.py:29
  89.8 7.0 %fusion.72 = f32[32,32,128]{2,1,0:T(8,128)S(1)} fusion(f32[1,32,2,128,128]{4,3,2,1,0:T(8,128)} %param.60, f32[32,2,32,128]{3,2,1,0:T(8,128)} %bitcast.677, pred[32,2]{1,0:T(8,128)(4,1)S(1)} %copy.65), kind=kOutput, calls=%fused_computation.66 | convolution fusion | flops 402915328 | bytes 5767232 | tf_op jit(solution)/shard_map/cbjk,bjik->cbi/dot_general | solution.py:31
  96.9 3.4 %fusion.111 = f32[32,32,128]{2,0,1:T(8,128)S(1)} fusion(f32[32,32,128]{2,1,0:T(8,128)S(1)} %fusion.72, f32[32,34,128]{2,0,1:T(8,128)S(1)} %copy-done.25, f32[1,32,128,128]{3,2,1,0:T(8,128)S(1)} %copy-done.10), kind=kOutput, calls=%fused_computation.79 | convolution fusion | flops 201457664 | bytes 3702784 | tf_op jit(solution)/shard_map/cbk,bik->cbi/dot_general | solution.py:29
  106.7 7.2 %fusion.75 = f32[32,32,128]{2,1,0:T(8,128)S(1)} fusion(f32[1,32,2,128,128]{4,3,2,1,0:T(8,128)} %param.60, f32[32,2,32,128]{3,2,1,0:T(8,128)} %bitcast.678, pred[32,2]{1,0:T(8,128)(4,1)S(1)} %copy.65), kind=kOutput, calls=%fused_computation.67 | convolution fusion | flops 402915328 | bytes 5767232 | tf_op jit(solution)/shard_map/cbjk,bjik->cbi/dot_general | solution.py:31
  114.0 3.4 %fusion.117 = f32[32,32,128]{2,0,1:T(8,128)S(1)} fusion(f32[32,32,128]{2,1,0:T(8,128)S(1)} %fusion.75, f32[32,34,128]{2,0,1:T(8,128)S(1)} %copy-done.31, f32[1,32,128,128]{3,2,1,0:T(8,128)S(1)} %copy-done.11), kind=kOutput, calls=%fused_computation.81 | convolution fusion | flops 201457664 | bytes 3702784 | tf_op jit(solution)/shard_map/cbk,bik->cbi/dot_general | solution.py:29
  132.2 3.9 %collective-permute-start.6 = (f32[32,1,128]{2,0,1:T(8,128)S(1)}, f32[32,1,128]{2,0,1:T(8,128)S(1)}, u32[]{:S(2)}, u32[]{:S(2)}) collective-permute-start(f32[32,1,128]{2,0,1:T(8,128)S(1)} %get-tuple-element.300), channel_id=1, source_target_pairs={{0,2},{2,4},{4,6},{6,8},{8,10},{10,12},{12,14},{14,16},{16,18},{18... | collective-permute-start | bytes 49160 | tf_op jit(solution)/shard_map/ppermute | solution.py:20
  136.1 7.0 %fusion.78 = f32[32,32,128]{2,1,0:T(8,128)S(1)} fusion(f32[1,32,2,128,128]{4,3,2,1,0:T(8,128)} %param.60, f32[32,2,32,128]{3,2,1,0:T(8,128)} %bitcast.674, pred[32,2]{1,0:T(8,128)(4,1)S(1)} %copy.65), kind=kOutput, calls=%fused_computation.68 | convolution fusion | flops 402915328 | bytes 5767232 | tf_op jit(solution)/shard_map/cbjk,bjik->cbi/dot_general | solution.py:31
  143.1 3.4 %fusion.57 = f32[32,32,128]{2,0,1:T(8,128)S(1)} fusion(f32[32,32,128]{2,1,0:T(8,128)S(1)} %fusion.78, f32[32,32,128]{2,0,1:T(8,128)S(1)} %get-tuple-element.299, f32[1,32,128,128]{3,2,1,0:T(8,128)S(1)} %copy-done.12), kind=kOutput, calls=%fused_computation.61 | convolution fusion | flops 201457664 | bytes 3670016 | tf_op jit(solution)/shard_map/cbk,bik->cbi/dot_general | solution.py:29
  158.6 20.9 %all-gather.3 = f32[32,32,128]{2,1,0:T(8,128)S(1)} all-gather(f32[2,32,128]{2,1,0:T(8,128)S(1)} %bitcast.683), channel_id=5, replica_groups=mesh['sub'=16,'coarse'=2] {'sub'}, dimensions={0}, use_global_device_ids=true | all-gather | bytes 557056 | tf_op jit(solution)/shard_map/all_gather | solution.py:91
  186.6 7.0 %fusion.81 = f32[32,32,128]{2,1,0:T(8,128)S(1)} fusion(f32[1,32,2,128,128]{4,3,2,1,0:T(8,128)} %param.60, f32[32,2,32,128]{3,2,1,0:T(8,128)} %bitcast.679, pred[32,2]{1,0:T(8,128)(4,1)S(1)} %copy.65), kind=kOutput, calls=%fused_computation.69 | convolution fusion | flops 402915328 | bytes 5767232 | tf_op jit(solution)/shard_map/cbjk,bjik->cbi/dot_general | solution.py:31
  193.7 3.4 %fusion.123 = f32[32,32,128]{2,0,1:T(8,128)S(1)} fusion(f32[32,32,128]{2,1,0:T(8,128)S(1)} %fusion.81, f32[1,32,128,128]{3,2,1,0:T(8,128)S(1)} %copy-done.13, f32[32,1,128]{2,0,1:T(8,128)S(1)} %copy-done.63, f32[32,32,128]{2,0,1:T(8,128)S(1)} %fusion.381, f32[32,1,128]{2,0,1:T(8,128)S(1)} %copy-done.58), kind=kOutput, calls=%fused_computation.83 | convolution fusion | flops 201875456 | bytes 3702784 | tf_op jit(solution)/shard_map/cbk,bik->cbi/dot_general | solution.py:29
  207.8 7.0 %fusion.84 = f32[32,32,128]{2,1,0:T(8,128)S(1)} fusion(f32[1,32,2,128,128]{4,3,2,1,0:T(8,128)} %param.60, f32[32,2,32,128]{3,2,1,0:T(8,128)} %bitcast.680, pred[32,2]{1,0:T(8,128)(4,1)S(1)} %copy.65), kind=kOutput, calls=%fused_computation.70 | convolution fusion | flops 402915328 | bytes 5767232 | tf_op jit(solution)/shard_map/cbjk,bjik->cbi/dot_general | solution.py:31
  214.8 3.6 %fusion.129 = f32[32,32,128]{2,0,1:T(8,128)S(1)} fusion(f32[32,32,128]{2,1,0:T(8,128)S(1)} %fusion.84, f32[32,34,128]{2,0,1:T(8,128)S(1)} %copy-done.35, f32[1,32,128,128]{3,2,1,0:T(8,128)S(1)} %copy-done.14), kind=kOutput, calls=%fused_computation.85 | convolution fusion | flops 201457664 | bytes 3702784 | tf_op jit(solution)/shard_map/cbk,bik->cbi/dot_general | solution.py:29
  224.8 7.0 %fusion.87 = f32[32,32,128]{2,1,0:T(8,128)S(1)} fusion(f32[1,32,2,128,128]{4,3,2,1,0:T(8,128)} %param.60, f32[32,2,32,128]{3,2,1,0:T(8,128)} %bitcast.681, pred[32,2]{1,0:T(8,128)(4,1)S(1)} %copy.65), kind=kOutput, calls=%fused_computation.71 | convolution fusion | flops 402915328 | bytes 5767232 | tf_op jit(solution)/shard_map/cbjk,bjik->cbi/dot_general | solution.py:31
  241.6 7.2 %fusion.90 = f32[32,32,128]{2,1,0:T(8,128)S(1)} fusion(f32[1,32,2,128,128]{4,3,2,1,0:T(8,128)} %param.60, f32[32,2,32,128]{3,2,1,0:T(8,128)} %bitcast.682, pred[32,2]{1,0:T(8,128)(4,1)S(1)} %copy.65), kind=kOutput, calls=%fused_computation.72 | convolution fusion | flops 402915328 | bytes 5767232 | tf_op jit(solution)/shard_map/cbjk,bjik->cbi/dot_general | solution.py:31
  270.4 3.9 %collective-permute-start.12 = (f32[32,1,128]{2,0,1:T(8,128)S(1)}, f32[32,1,128]{2,0,1:T(8,128)S(1)}, u32[]{:S(2)}, u32[]{:S(2)}) collective-permute-start(f32[32,1,128]{2,0,1:T(8,128)S(1)} %get-tuple-element.298), channel_id=1, source_target_pairs={{0,2},{2,4},{4,6},{6,8},{8,10},{10,12},{12,14},{14,16},{16,18},{18... | collective-permute-start | bytes 49160 | tf_op jit(solution)/shard_map/ppermute | solution.py:20
  274.4 7.0 %fusion.93 = f32[32,32,128]{2,1,0:T(8,128)S(1)} fusion(f32[1,32,2,128,128]{4,3,2,1,0:T(8,128)} %param.60, f32[32,2,32,128]{3,2,1,0:T(8,128)} %bitcast.673, pred[32,2]{1,0:T(8,128)(4,1)S(1)} %copy.65), kind=kOutput, calls=%fused_computation.73 | convolution fusion | flops 402915328 | bytes 5767232 | tf_op jit(solution)/shard_map/cbjk,bjik->cbi/dot_general | solution.py:31
  281.4 3.4 %fusion.63 = f32[32,32,128]{2,0,1:T(8,128)S(1)} fusion(f32[32,32,128]{2,1,0:T(8,128)S(1)} %fusion.93, f32[32,32,128]{2,0,1:T(8,128)S(1)} %copy-done.3, f32[1,32,128,128]{3,2,1,0:T(8,128)S(1)} %copy-done.17), kind=kOutput, calls=%fused_computation.63 | convolution fusion | flops 201457664 | bytes 3670016 | tf_op jit(solution)/shard_map/cbk,bik->cbi/dot_general | solution.py:29
  (375 shorter events, 123.4 us)
Async XLA Ops:
  0.6 15.0 %copy-start = (f32[1,128,32,128]{3,2,1,0:T(8,128)S(1)}, f32[1,128,32,128]{3,2,1,0:T(8,128)}, u32[]{:S(2)}) copy-start(f32[1,128,32,128]{3,2,1,0:T(8,128)} %param.63) | copy-start | bytes 6291460
  0.6 15.0 %copy-start.36 = (f32[1,32,32,128]{3,2,1,0:T(8,128)S(1)}, f32[1,32,32,128]{3,2,1,0:T(8,128)}, u32[]{:S(2)}) copy-start(f32[1,32,32,128]{3,2,1,0:T(8,128)} %param.58) | copy-start | bytes 1572868
  0.7 14.7 %copy-start.106 = (s32[1,32,2]{1,2,0:T(2,128)S(1)}, s32[1,32,2]{1,2,0:T(2,128)}, u32[]{:S(2)}) copy-start(s32[1,32,2]{1,2,0:T(2,128)} %param.61) | copy-start | bytes 772
  2.4 61.4 %collective-permute-start.3 = (f32[1,2,128,128]{3,2,1,0:T(8,128)}, f32[1,2,128,128]{3,2,1,0:T(8,128)S(1)}, u32[]{:S(2)}, u32[]{:S(2)}) collective-permute-start(f32[1,2,128,128]{3,2,1,0:T(8,128)} %maximum_bitcast_fusion.1), channel_id=1, source_target_pairs={{2,0},{4,2},{6,4},{8,6},{10,8},{12,10},{14,12},{16,14},{18,16},{20... | collective-permute-start | bytes 393224 | tf_op jit(solution)/shard_map/ppermute | solution.py:23
  5.1 41.9 %copy-start.105 = (s32[1,6]{1,0:T(1,128)S(1)}, s32[1,6]{1,0:T(1,128)}, u32[]{:S(2)}) copy-start(s32[1,6]{1,0:T(1,128)} %param.65) | copy-start | bytes 76
  5.1 60.6 %collective-permute-start.2 = (f32[1,2,128,128]{3,2,1,0:T(8,128)}, f32[1,2,128,128]{3,2,1,0:T(8,128)S(1)}, u32[]{:S(2)}, u32[]{:S(2)}) collective-permute-start(f32[1,2,128,128]{3,2,1,0:T(8,128)} %maximum_bitcast_fusion), channel_id=1, source_target_pairs={{0,2},{2,4},{4,6},{6,8},{8,10},{10,12},{12,14},{14,16},{16,18},{18... | collective-permute-start | bytes 393224 | tf_op jit(solution)/shard_map/ppermute | solution.py:20
  11.1 37.8 %collective-permute-start = (f32[32,1,128]{2,0,1:T(8,128)S(1)}, f32[32,1,128]{2,0,1:T(8,128)S(1)}, u32[]{:S(2)}, u32[]{:S(2)}) collective-permute-start(f32[32,1,128]{2,0,1:T(8,128)S(1)} %get-tuple-element.309), channel_id=1, source_target_pairs={{0,2},{2,4},{4,6},{6,8},{8,10},{10,12},{12,14},{14,16},{16,18},{18... | collective-permute-start | bytes 49160 | tf_op jit(solution)/shard_map/ppermute | solution.py:20
  13.5 35.3 %collective-permute-start.1 = (f32[32,1,128]{2,0,1:T(8,128)S(1)}, f32[32,1,128]{2,0,1:T(8,128)S(1)}, u32[]{:S(2)}, u32[]{:S(2)}) collective-permute-start(f32[32,1,128]{2,0,1:T(8,128)S(1)} %get-tuple-element.310), channel_id=1, source_target_pairs={{2,0},{4,2},{6,4},{8,6},{10,8},{12,10},{14,12},{16,14},{18,16},{20... | collective-permute-start | bytes 49160 | tf_op jit(solution)/shard_map/ppermute | solution.py:23
  15.6 31.9 %copy-start.45 = (f32[1,6,128,128]{3,2,1,0:T(8,128)S(1)}, f32[1,6,128,128]{3,2,1,0:T(8,128)}, u32[]{:S(2)}) copy-start(f32[1,6,128,128]{3,2,1,0:T(8,128)} %param.64) | copy-start | bytes 1179652
  106.7 7.2 %copy-start.11 = (f32[1,32,128,128]{3,2,1,0:T(8,128)S(1)}, f32[1,32,128,128]{3,2,1,0:T(8,128)}, u32[]{:S(2)}) copy-start(f32[1,32,128,128]{3,2,1,0:T(8,128)} %param.59) | copy-start | bytes 6291460
  106.7 7.2 %copy-start.31 = (f32[32,34,128]{2,0,1:T(8,128)S(1)}, f32[32,34,128]{2,0,1:T(8,128)}, u32[]{:S(2)}) copy-start(f32[32,34,128]{2,0,1:T(8,128)} %copy-done.30) | copy-start | bytes 1671172
  119.4 6.7 %collective-permute-start.4 = (f32[32,1,128]{2,0,1:T(8,128)S(1)}, f32[32,1,128]{2,0,1:T(8,128)S(1)}, u32[]{:S(2)}, u32[]{:S(2)}) collective-permute-start(f32[32,1,128]{2,0,1:T(8,128)S(1)} %get-tuple-element.306), channel_id=1, source_target_pairs={{0,2},{2,4},{4,6},{6,8},{8,10},{10,12},{12,14},{14,16},{16,18},{18... | collective-permute-start | bytes 49160 | tf_op jit(solution)/shard_map/ppermute | solution.py:20
  123.6 5.1 %collective-permute-start.5 = (f32[32,1,128]{2,0,1:T(8,128)S(1)}, f32[32,1,128]{2,0,1:T(8,128)S(1)}, u32[]{:S(2)}, u32[]{:S(2)}) collective-permute-start(f32[32,1,128]{2,0,1:T(8,128)S(1)} %get-tuple-element.305), channel_id=1, source_target_pairs={{2,0},{4,2},{6,4},{8,6},{10,8},{12,10},{14,12},{16,14},{18,16},{20... | collective-permute-start | bytes 49160 | tf_op jit(solution)/shard_map/ppermute | solution.py:23
  130.3 16.6 %collective-permute-start.7 = (f32[32,1,128]{2,0,1:T(8,128)S(1)}, f32[32,1,128]{2,0,1:T(8,128)S(1)}, u32[]{:S(2)}, u32[]{:S(2)}) collective-permute-start(f32[32,1,128]{2,0,1:T(8,128)S(1)} %slice.931), channel_id=1, source_target_pairs={{2,0},{4,2},{6,4},{8,6},{10,8},{12,10},{14,12},{16,14},{18,16},{20... | collective-permute-start | bytes 49160 | tf_op jit(solution)/shard_map/ppermute | solution.py:23
  132.2 14.4 %collective-permute-start.6 = (f32[32,1,128]{2,0,1:T(8,128)S(1)}, f32[32,1,128]{2,0,1:T(8,128)S(1)}, u32[]{:S(2)}, u32[]{:S(2)}) collective-permute-start(f32[32,1,128]{2,0,1:T(8,128)S(1)} %get-tuple-element.300), channel_id=1, source_target_pairs={{0,2},{2,4},{4,6},{6,8},{8,10},{10,12},{12,14},{14,16},{16,18},{18... | collective-permute-start | bytes 49160 | tf_op jit(solution)/shard_map/ppermute | solution.py:20
  147.4 32.6 %copy-start.46 = (f32[1,6,128,128]{3,2,1,0:T(8,128)S(1)}, f32[1,6,128,128]{3,2,1,0:T(8,128)}, u32[]{:S(2)}) copy-start(f32[1,6,128,128]{3,2,1,0:T(8,128)} %param.64) | copy-start | bytes 1179652
  153.6 27.6 %collective-permute-start.8 = (f32[32,1,128]{2,0,1:T(8,128)S(1)}, f32[32,1,128]{2,0,1:T(8,128)S(1)}, u32[]{:S(2)}, u32[]{:S(2)}) collective-permute-start(f32[32,1,128]{2,0,1:T(8,128)S(1)} %get-tuple-element.307), channel_id=1, source_target_pairs={{0,2},{2,4},{4,6},{6,8},{8,10},{10,12},{12,14},{14,16},{16,18},{18... | collective-permute-start | bytes 49160 | tf_op jit(solution)/shard_map/ppermute | solution.py:20
  156.7 24.5 %collective-permute-start.9 = (f32[32,1,128]{2,0,1:T(8,128)S(1)}, f32[32,1,128]{2,0,1:T(8,128)S(1)}, u32[]{:S(2)}, u32[]{:S(2)}) collective-permute-start(f32[32,1,128]{2,0,1:T(8,128)S(1)} %get-tuple-element.308), channel_id=1, source_target_pairs={{2,0},{4,2},{6,4},{8,6},{10,8},{12,10},{14,12},{16,14},{18,16},{20... | collective-permute-start | bytes 49160 | tf_op jit(solution)/shard_map/ppermute | solution.py:23
  241.6 7.2 %copy-start.16 = (f32[1,32,128,128]{3,2,1,0:T(8,128)S(1)}, f32[1,32,128,128]{3,2,1,0:T(8,128)}, u32[]{:S(2)}) copy-start(f32[1,32,128,128]{3,2,1,0:T(8,128)} %param.59) | copy-start | bytes 6291460
  241.6 7.2 %copy-start.29 = (f32[32,34,128]{2,0,1:T(8,128)S(1)}, f32[32,34,128]{2,0,1:T(8,128)}, u32[]{:S(2)}) copy-start(f32[32,34,128]{2,0,1:T(8,128)} %copy-done.28) | copy-start | bytes 1671172
  254.4 6.7 %collective-permute-start.10 = (f32[32,1,128]{2,0,1:T(8,128)S(1)}, f32[32,1,128]{2,0,1:T(8,128)S(1)}, u32[]{:S(2)}, u32[]{:S(2)}) collective-permute-start(f32[32,1,128]{2,0,1:T(8,128)S(1)} %get-tuple-element.304), channel_id=1, source_target_pairs={{0,2},{2,4},{4,6},{6,8},{8,10},{10,12},{12,14},{14,16},{16,18},{18... | collective-permute-start | bytes 49160 | tf_op jit(solution)/shard_map/ppermute | solution.py:20
  258.7 5.1 %collective-permute-start.11 = (f32[32,1,128]{2,0,1:T(8,128)S(1)}, f32[32,1,128]{2,0,1:T(8,128)S(1)}, u32[]{:S(2)}, u32[]{:S(2)}) collective-permute-start(f32[32,1,128]{2,0,1:T(8,128)S(1)} %get-tuple-element.303), channel_id=1, source_target_pairs={{2,0},{4,2},{6,4},{8,6},{10,8},{12,10},{14,12},{16,14},{18,16},{20... | collective-permute-start | bytes 49160 | tf_op jit(solution)/shard_map/ppermute | solution.py:23
  268.5 16.6 %collective-permute-start.13 = (f32[32,1,128]{2,0,1:T(8,128)S(1)}, f32[32,1,128]{2,0,1:T(8,128)S(1)}, u32[]{:S(2)}, u32[]{:S(2)}) collective-permute-start(f32[32,1,128]{2,0,1:T(8,128)S(1)} %slice.969), channel_id=1, source_target_pairs={{2,0},{4,2},{6,4},{8,6},{10,8},{12,10},{14,12},{16,14},{18,16},{20... | collective-permute-start | bytes 49160 | tf_op jit(solution)/shard_map/ppermute | solution.py:23
  270.4 14.4 %collective-permute-start.12 = (f32[32,1,128]{2,0,1:T(8,128)S(1)}, f32[32,1,128]{2,0,1:T(8,128)S(1)}, u32[]{:S(2)}, u32[]{:S(2)}) collective-permute-start(f32[32,1,128]{2,0,1:T(8,128)S(1)} %get-tuple-element.298), channel_id=1, source_target_pairs={{0,2},{2,4},{4,6},{6,8},{8,10},{10,12},{12,14},{14,16},{16,18},{18... | collective-permute-start | bytes 49160 | tf_op jit(solution)/shard_map/ppermute | solution.py:20
  (97 other events, 370.8 us)
where the time goes:
time: 292 us; the launch traced here: 287 us
  matrix products  139 us (48%)
  blocking collectives  52.4 us (18%)
  local copies, waits for them, and re-layouts  46 us (16%)
  starting transfers between devices  36.1 us (12%)
  waiting for transfers between devices  5.32 us (2%)
  other arithmetic  5.21 us (2%)
  between operations  3.31 us (1%)
    dot_general x10, matrix products, own_rows(): jnp.einsum('cbjk,bjik->cbi', picked, offs, precision=highest)  70.6 us
    all_gather x2, blocking collectives, per_device(): piece = lax.all_gather(across[None], 'sub', axis=0, tiled=True)  45.7 us
    dot_general x10, matrix products, own_rows(): result = jnp.einsum('cbk,bik->cbi', own, diag, precision=highest)  34.8 us
    gather x10, local copies, waits for them, and re-layouts, own_rows(): picked = jnp.take(own, index, axis=1)  24.4 us
    ppermute x7, starting transfers between devices, padded_2(): lax.ppermute(lax.slice_in_dim(block, block.shape[dim] - width, None, axis...  21.7 us
    ppermute x7, starting transfers between devices, padded_2(): lax.ppermute(lax.slice_in_dim(block, 0, width, axis=dim), axis, backward)  14.3 us
    unnamed x229, local copies, waits for them, and re-layouts  14.3 us
    all_gather x2, blocking collectives, per_device(): across = lax.all_gather(coeffs[None], 'coarse', axis=0, tiled=True)  6.69 us
  transfers between devices with their start and end apart: 14, of which 2 were waited for; matrix products, arithmetic and copies ran while one was open for 18% of the time, Pallas kernels for 0%

commit v1 on v0

v1 whole, which is shorter than its diff:
```python
import functools

import jax
import jax.numpy as jnp
from jax import lax
from jax.experimental import pallas as pl
from jax.experimental.pallas import tpu as pltpu
from jax.sharding import PartitionSpec as P

ORDER = 5
ITERS = 2
THETA = 5.0
DELTA = 4.0
F32 = jnp.float32
BF16 = jnp.bfloat16
MESH = pl.DeviceIdType.MESH


def cheb_coefs():
    sigma = THETA / DELTA
    rho = 1.0 / sigma
    out = []
    for _ in range(ORDER - 1):
        nxt = 1.0 / (2.0 * sigma - rho)
        out.append((nxt * rho, 2.0 * nxt / DELTA))
        rho = nxt
    return out


def halves(v):
    hi = v.astype(BF16)
    lo = (v - hi.astype(F32)).astype(BF16)
    return hi, lo


def dot_nt(x, w):
    return lax.dot_general(x, w, (((1,), (1,)), ((), ())), preferred_element_type=F32)


def dot_nn(x, w):
    return lax.dot_general(x, w, (((1,), (0,)), ((), ())), preferred_element_type=F32)


def kernel(
    ns, nc, nb, cols, bs, ncb,
    loads, diag, offs, oidx, couple, basis, cblk, cidx,
    sol, res,
    f_loads, f_diag, f_offs, f_couple, f_basis, f_cblk,
    w, wc, wt, bw, cw,
    r, d, z, ua, ub, ur,
    gath0, gath1, op_in, r_in, e_in, e_out,
    lsem, op_s, op_r, rh_s, rh_r, e_s, e_r, g1_s, g1_r, g2_s, g2_r, g3_s, g3_r,
):
    me_s = lax.axis_index("sub")
    me_x = lax.axis_index("coarse")
    core = lax.rem(me_s, 2)
    h = me_s // 2
    half = ns // 2
    partner = me_s + 1 - 2 * core
    has_l = me_s > 0
    has_r = me_s < ns - 1
    nb2 = nb // 2
    left, right = nb, nb + 1

    ld = [
        pltpu.make_async_copy(loads, f_loads, lsem.at[0]),
        pltpu.make_async_copy(basis, f_basis, lsem.at[1]),
        pltpu.make_async_copy(couple, f_couple, lsem.at[2]),
        pltpu.make_async_copy(diag, f_diag, lsem.at[3]),
        pltpu.make_async_copy(offs, f_offs, lsem.at[4]),
        pltpu.make_async_copy(cblk, f_cblk, lsem.at[5]),
    ]
    for c in ld:
        c.start()

    def remote(src, dst, ss, rs, s, x):
        return pltpu.make_async_remote_copy(
            src_ref=src, dst_ref=dst, send_sem=ss, recv_sem=rs,
            device_id={"sub": s, "coarse": x}, device_id_type=MESH,
        )

    barrier = pltpu.get_barrier_semaphore()

    def greet(s, x):
        pl.semaphore_signal(
            barrier, inc=1, device_id={"sub": s, "coarse": x}, device_id_type=MESH
        )

    for k in range(1, half):
        greet(core + 2 * lax.rem(h + k, half), me_x)
    for k in range(1, nc):
        greet(me_s, lax.rem(me_x + k, nc))

    @pl.when(has_l)
    def _():
        greet(me_s - 1, me_x)

    @pl.when(has_r)
    def _():
        greet(me_s + 1, me_x)

    def put(ref, b, v):
        hi, lo = halves(v)
        ref[b, 0:cols, :] = hi
        ref[b, cols : 2 * cols, :] = lo

    def fold(o):
        return (o[:cols, :bs] + o[:cols, bs:]) + (o[cols:, :bs] + o[cols:, bs:])

    ld[0].wait()

    def init_r(b, carry):
        v = f_loads[pl.ds(b, cols, stride=nb), :]
        r[b] = v
        put(ur, b, v)
        return carry

    lax.fori_loop(0, nb, init_r, 0)
    ld[1].wait()

    def init_bw(t, carry):
        for p in range(2):
            v = f_basis[pl.ds(2 * t + p, bs, stride=nb), :]
            hi, lo = halves(v)
            bw[t, 0:bs, p * bs : (p + 1) * bs] = hi
            bw[t, bs : 2 * bs, p * bs : (p + 1) * bs] = lo
        return carry

    lax.fori_loop(0, nb2, init_bw, 0)

    pl.semaphore_wait(barrier, half - 1 + nc - 1 + has_l.astype(jnp.int32) + has_r.astype(jnp.int32))

    def op_copies(to_left):
        b = 0 if to_left else nb - 1
        side = 1 if to_left else 0
        s = me_s - 1 if to_left else me_s + 1
        return [
            remote(f_diag.at[b], op_in.at[side, 0], op_s.at[side, 0], op_r.at[side, 0], s, me_x),
            remote(
                f_couple.at[0 if to_left else 1], op_in.at[side, 1],
                op_s.at[side, 1], op_r.at[side, 1], s, me_x,
            ),
        ]

    def r_copy(it, to_left):
        b = 0 if to_left else nb - 1
        side = 1 if to_left else 0
        s = me_s - 1 if to_left else me_s + 1
        return [remote(r.at[b], r_in.at[it, side], rh_s.at[it, side], rh_r.at[it, side], s, me_x)]

    def e_copy(it, to_left):
        side = 1 if to_left else 0
        s = me_s - 1 if to_left else me_s + 1
        return [
            remote(
                e_out.at[it, side], e_in.at[it, side], e_s.at[it, side], e_r.at[it, side], s, me_x
            )
        ]

    def start_both(make):
        @pl.when(has_l)
        def _():
            for c in make(True):
                c.start()

        @pl.when(has_r)
        def _():
            for c in make(False):
                c.start()

    def wait_both(make):
        @pl.when(has_l)
        def _():
            for c in make(True):
                c.wait_send()
            for c in make(False):
                c.wait_recv()

        @pl.when(has_r)
        def _():
            for c in make(False):
                c.wait_send()
            for c in make(True):
                c.wait_recv()

    for side, has in ((0, has_l), (1, has_r)):

        @pl.when(jnp.logical_not(has))
        def _():
            op_in[side] = jnp.zeros_like(op_in[side])
            for it in range(ITERS):
                r_in[it, side] = jnp.zeros_like(r_in[it, side])
                e_in[it, side] = jnp.zeros_like(e_in[it, side])

    own = me_x * half + h
    gath = (gath0, gath1)

    def g1(it):
        return [
            remote(
                gath[it].at[core, own], gath[it].at[core, own],
                g1_s.at[it, k - 1], g1_r.at[it, k - 1],
                core + 2 * lax.rem(h + k, half), me_x,
            )
            for k in range(1, half)
        ]

    def g2(it):
        span = pl.ds(me_x * half, half)
        return [
            remote(
                gath[it].at[core, span], gath[it].at[core, span],
                g2_s.at[it, k - 1], g2_r.at[it, k - 1],
                me_s, lax.rem(me_x + k, nc),
            )
            for k in range(1, nc)
        ]

    def g3(it):
        return [
            remote(
                gath[it].at[core], gath[it].at[core], g3_s.at[it], g3_r.at[it], partner, me_x
            )
        ]

    def start(copies):
        for c in copies:
            c.start()

    def wait(copies):
        for c in copies:
            c.wait()

    def coeffs(it):
        def body(q, acc):
            for p in range(4):
                t = 4 * q + p
                x = jnp.concatenate([ur[2 * t], ur[2 * t + 1]], axis=1)
                acc = acc + dot_nt(x, bw[t])
            return acc

        acc = lax.fori_loop(0, nb2 // 4, body, jnp.zeros((2 * cols, 2 * bs), F32))
        gath[it][core, own] = fold(acc)

    def row(u, b):
        x = jnp.concatenate([u[b], u[oidx[b, 0]], u[oidx[b, 1]]], axis=1)
        return fold(dot_nt(x, w[b]))

    GROUP = 6

    def middle(u, emit):
        def body(q, carry):
            rows = [1 + q * GROUP + p for p in range(GROUP)]
            ys = [row(u, b) for b in rows]
            emit(rows, ys)
            return carry

        lax.fori_loop(0, (nb - 2) // GROUP, body, 0)

    def first_last(u):
        y0 = row(u, 0) + fold(dot_nt(u[left], wc[0]))
        y1 = row(u, nb - 1) + fold(dot_nt(u[right], wc[1]))
        return y0, y1

    def outer(u):
        yl = fold(dot_nt(jnp.concatenate([u[left], u[0]], axis=1), wt[0]))
        yr = fold(dot_nt(jnp.concatenate([u[right], u[nb - 1]], axis=1), wt[1]))
        return yl, yr

    coefs = cheb_coefs()

    def emit_step(k, unew):
        ca, cc = coefs[k]

        def emit(rows, ys):
            out = []
            for b, y in zip(rows, ys):
                rv = r[b]
                if k == 0:
                    dv = rv * (1.0 / THETA)
                    zv = dv
                    y = y * (1.0 / THETA)
                else:
                    dv = d[b]
                    zv = z[b]
                dv = ca * dv + cc * (rv - y)
                out.append((dv, zv + dv))
            for b, (dv, zv) in zip(rows, out):
                if k + 2 < ORDER:
                    d[b] = dv
                    put(unew, b, zv)
                z[b] = zv

        return emit

    def ends_step(k, u, unew):
        yl, yr = outer(u)
        y0, y1 = first_last(u)
        emit_step(k, unew)([0, nb - 1, left, right], [y0, y1, yl, yr])

    def iteration(it):
        last = it + 1 == ITERS
        middle(ur, emit_step(0, ua))
        wait_both(functools.partial(r_copy, it))
        for side, b in ((0, left), (1, right)):
            v = r_in[it, side]
            r[b] = v
            put(ur, b, v)
        ends_step(0, ur, ua)
        wait(g1(it))
        start(g2(it))
        middle(ua, emit_step(1, ub))
        ends_step(1, ua, ub)
        middle(ub, emit_step(2, ua))
        ends_step(2, ub, ua)
        wait(g2(it))
        start(g3(it))
        ends_step(3, ua, ub)
        middle(ua, emit_step(3, ub))
        wait(g3(it))

        xs = []
        for j in range(ncb):
            g = cidx[j]
            s = g // nc
            x = lax.rem(g, nc)
            hi, lo = halves(gath[it][lax.rem(s, 2), x * half + s // 2])
            xs.append(jnp.concatenate([hi, lo], axis=0))
        csol = fold(dot_nt(jnp.concatenate(xs, axis=1), cw[...]))
        hi, lo = halves(csol)
        cx = jnp.concatenate([hi, lo], axis=0)
        cx = jnp.concatenate([cx, cx], axis=1)

        def spread(t):
            o = dot_nn(cx, bw[t])
            o = o[:cols] + o[cols:]
            return o[:, :bs], o[:, bs:]

        def keep(b, v):
            sol[b] = v if it == 0 else sol[b] + v
            put(ub, b, v)

        a0, a1 = spread(0)
        b0, b1 = spread(nb2 - 1)
        edge_l = z[0] + a0
        edge_r = z[nb - 1] + b1
        e_out[it, 1, 0] = z[left]
        e_out[it, 1, 1] = edge_l
        e_out[it, 0, 0] = z[right]
        e_out[it, 0, 1] = edge_r
        start_both(functools.partial(e_copy, it))
        keep(1, z[1] + a1)
        keep(nb - 2, z[nb - 2] + b0)

        def spread_body(q, carry):
            for p in range(2):
                t = 1 + 2 * q + p
                v0, v1 = spread(t)
                keep(2 * t, z[2 * t] + v0)
                keep(2 * t + 1, z[2 * t + 1] + v1)
            return carry

        lax.fori_loop(0, (nb2 - 2) // 2, spread_body, 0)
        wait_both(functools.partial(e_copy, it))
        keep(0, edge_l + e_in[it, 0, 0])
        keep(nb - 1, edge_r + e_in[it, 1, 0])
        put(ub, left, e_in[it, 0, 1] + z[left])
        put(ub, right, e_in[it, 1, 1] + z[right])

        def emit_res(rows, ys):
            vals = [r[b] - y for b, y in zip(rows, ys)]
            for b, v in zip(rows, vals):
                if last:
                    res[b] = v
                else:
                    r[b] = v
                    put(ur, b, v)

        emit_res([0, nb - 1], list(first_last(ub)))
        if not last:
            start_both(functools.partial(r_copy, it + 1))
        middle(ub, emit_res)
        if not last:
            coeffs(it + 1)
            start(g1(it + 1))

    start_both(functools.partial(r_copy, 0))
    coeffs(0)
    start(g1(0))
    ld[2].wait()
    ld[3].wait()
    start_both(op_copies)
    ld[4].wait()

    def init_w(b, carry):
        for j, v in enumerate((f_diag[b], f_offs[b, 0], f_offs[b, 1])):
            hi, lo = halves(v)
            w[b, 0:bs, j * bs : (j + 1) * bs] = hi
            w[b, bs : 2 * bs, j * bs : (j + 1) * bs] = lo
        return carry

    lax.fori_loop(0, nb, init_w, 0)
    for j in range(2):
        hi, lo = halves(f_couple[j])
        wc[j, 0:bs, :] = hi
        wc[j, bs : 2 * bs, :] = lo
    ld[5].wait()
    for j in range(ncb):
        hi, lo = halves(f_cblk[j])
        cw[0:bs, j * bs : (j + 1) * bs] = hi
        cw[bs : 2 * bs, j * bs : (j + 1) * bs] = lo
    wait_both(op_copies)
    for side in range(2):
        for j in range(2):
            hi, lo = halves(op_in[side, j])
            wt[side, 0:bs, j * bs : (j + 1) * bs] = hi
            wt[side, bs : 2 * bs, j * bs : (j + 1) * bs] = lo

    for it in range(ITERS):
        iteration(it)


def per_device(ns, nc, loads, diag, offs, oidx, couple, basis, cblk, cidx):
    _, cols, nb, bs = loads.shape
    k = basis.shape[1]
    ncb = cblk.shape[1]
    half = ns // 2
    anyspace = pl.BlockSpec(memory_space=pl.ANY)
    smem = pl.BlockSpec(memory_space=pltpu.SMEM)
    vmem = pl.BlockSpec(memory_space=pltpu.VMEM)
    field = (nb + 2, cols, bs)
    ufield = (nb + 2, 2 * cols, bs)
    dma = pltpu.SemaphoreType.DMA
    out = jax.ShapeDtypeStruct((nb, cols, bs), F32)
    sol, res = pl.pallas_call(
        functools.partial(kernel, ns, nc, nb, cols, bs, ncb),
        out_shape=(out, out),
        in_specs=[anyspace, anyspace, anyspace, smem, anyspace, anyspace, anyspace, smem],
        out_specs=(vmem, vmem),
        scratch_shapes=[
            pltpu.VMEM((cols * nb, bs), F32),
            pltpu.VMEM((nb, bs, bs), F32),
            pltpu.VMEM((nb, 2, bs, bs), F32),
            pltpu.VMEM((2, bs, bs), F32),
            pltpu.VMEM((k * nb, bs), F32),
            pltpu.VMEM((ncb, bs, bs), F32),
            pltpu.VMEM((nb, 2 * bs, 3 * bs), BF16),
            pltpu.VMEM((2, 2 * bs, bs), BF16),
            pltpu.VMEM((2, 2 * bs, 2 * bs), BF16),
            pltpu.VMEM((nb // 2, 2 * bs, 2 * bs), BF16),
            pltpu.VMEM((2 * bs, ncb * bs), BF16),
            pltpu.VMEM(field, F32),
            pltpu.VMEM(field, F32),
            pltpu.VMEM(field, F32),
            pltpu.VMEM(ufield, BF16),
            pltpu.VMEM(ufield, BF16),
            pltpu.VMEM(ufield, BF16),
            pltpu.VMEM((2, nc * half, cols, bs), F32),
            pltpu.VMEM((2, nc * half, cols, bs), F32),
            pltpu.VMEM((2, 2, bs, bs), F32),
            pltpu.VMEM((ITERS, 2, cols, bs), F32),
            pltpu.VMEM((ITERS, 2, 2, cols, bs), F32),
            pltpu.VMEM((ITERS, 2, 2, cols, bs), F32),
            dma((6,)),
            dma((2, 2)),
            dma((2, 2)),
            dma((ITERS, 2)),
            dma((ITERS, 2)),
            dma((ITERS, 2)),
            dma((ITERS, 2)),
            dma((ITERS, half - 1)),
            dma((ITERS, half - 1)),
            dma((ITERS, nc - 1)),
            dma((ITERS, nc - 1)),
            dma((ITERS,)),
            dma((ITERS,)),
        ],
        compiler_params=pltpu.CompilerParams(
            collective_id=0, has_side_effects=True, vmem_limit_bytes=56 * 1024 * 1024
        ),
    )(
        loads.reshape(cols * nb, bs), diag[0], offs[0], oidx[0], couple[0],
        basis.reshape(k * nb, bs), cblk[0], cidx[0],
    )
    return sol.transpose(1, 0, 2)[None], res.transpose(1, 0, 2)[None]


def solution(mesh):
    lead = ("sub", "coarse")
    in_specs = (
        P(lead, None, None, None),
        P(lead, None, None, None),
        P(lead, None, None, None, None),
        P(lead, None, None),
        P(lead, None, None, None),
        P(lead, None, None, None),
        P(lead, None, None, None),
        P(lead, None),
    )
    out_specs = (P(lead, None, None, None), P(lead, None, None, None))
    return jax.shard_map(
        functools.partial(per_device, mesh.shape["sub"], mesh.shape["coarse"]),
        mesh=mesh, in_specs=in_specs, out_specs=out_specs, check_vma=False,
    )
```

time: 292 us -> 59.6 us (0.20); the launches traced: 287 us -> 59.3 us
  matrix products: 139 us -> 0 us
  Pallas kernels: 0 us -> 53 us
  blocking collectives: 52.4 us -> 0 us
  local copies, waits for them, and re-layouts: 46 us -> 5.65 us
  starting transfers between devices: 36.1 us -> 0 us
  waiting for transfers between devices: 5.32 us -> 0 us
  other arithmetic: 5.21 us -> 0 us
    dot_general x80 -> x0, matrix products: 139 us -> none  [the longest x10 70.6 us: own_rows(): jnp.einsum('cbjk,bjik->cbi', picked, offs, precision=highest)]
    pallas_call x0 -> x1, Pallas kernels: none -> 53 us  [per_device(): pl.pallas_call(functools.partial(kernel, ns, nc, nb, cols, bs, ncb), out_...]
    all_gather x4 -> x0, blocking collectives: 52.4 us -> none  [the longest x2 45.7 us: per_device(): piece = lax.all_gather(across[None], 'sub', axis=0, tiled=True)]
    ppermute x14 -> x0, starting transfers between devices: 36.1 us -> none  [the longest x7 21.7 us: padded_2(): lax.ppermute(lax.slice_in_dim(block, block.shape[dim] - width, None, axis...]
    gather x10 -> x0, local copies, waits for them, and re-layouts: 24.4 us -> none  [own_rows(): picked = jnp.take(own, index, axis=1)]
    unnamed x229 -> x2, local copies, waits for them, and re-layouts: 14.3 us -> 4.28 us
    slice x15 -> x0, local copies, waits for them, and re-layouts: 6.96 us -> none  [the longest x8 5.83 us: padded_rows(): padded[:, 1:-1]]
    ppermute x14 -> x0, waiting for transfers between devices: 5.32 us -> none  [the longest x7 5.3 us: padded_2(): lax.ppermute(lax.slice_in_dim(block, 0, width, axis=dim), axis, backward)]
  transfers between devices with their start and end apart: 14 -> 0, of which waited for: 2 -> 0; matrix products, arithmetic and copies ran while one was open for 18% -> 0% of each run, Pallas kernels for 0% -> 0%
where the time goes in v1:
time: 59.6 us; the launch traced here: 59.3 us
  Pallas kernels  53 us (89%)
  local copies, waits for them, and re-layouts  5.65 us (9%)
  between operations  0.64 us (1%)
    pallas_call x1, Pallas kernels, per_device(): pl.pallas_call(functools.partial(kernel, ns, nc, nb, cols, bs, ncb), out_...  53 us
    unnamed x2, local copies, waits for them, and re-layouts  4.28 us
    squeeze x1, local copies, waits for them, and re-layouts, per_device(): oidx[0]  1.36 us

profile of v1, /device:TPU:1, one launch (start us, length us, event | category | flops | bytes accessed | tf_op | source)
XLA Modules:
  0.0 59.3 jit_solution(4827157081561198908)
XLA Ops:
  0.6 1.4 %copy.10.oidx = s32[32,2]{1,0:T(8,128)} copy(s32[32,2]{0,1:T(2,128)} %bitcast.22) | data formatting | bytes 512 | tf_op jit(solution)/shard_map/squeeze | solution.py:482
  2.0 53.0 %shard_map.95 = (f32[32,32,128]{2,1,0:T(8,128)}, f32[32,32,128]{2,1,0:T(8,128)}) custom-call(f32[1024,128]{1,0:T(8,128)} %bitcast.17, f32[32,128,128]{2,1,0:T(8,128)} %bitcast.15, f32[32,2,128,128]{3,2,1,0:T(8,128)} %bitcast.14, s32[32,2]{1,0:T(8,128)} %copy.10.oidx, f32[2,128,128]{2,1,0:T(8,128)} %bitcast.21, f32[4096,128]{1,0:T(8,128)} %bitcast.16, ...), custom_call_target="tpu_custom_call" | custom-call | tf_op jit(solution)/shard_map/pallas_call | solution.py:435
  55.0 2.1 %copy.11 = f32[1,32,32,128]{3,2,1,0:T(8,128)} copy(f32[1,32,32,128]{3,1,2,0:T(8,128)} %bitcast.19) | data formatting | bytes 1048576
  57.2 2.1 %copy.12 = f32[1,32,32,128]{3,2,1,0:T(8,128)} copy(f32[1,32,32,128]{3,1,2,0:T(8,128)} %bitcast.18) | data formatting | bytes 1048576

commit v2 on v1

--- a/solution.py
+++ b/solution.py
@@ -243,28 +243,32 @@
         gath[it][core, own] = fold(acc)
 
     def row(u, b):
-        x = jnp.concatenate([u[b], u[oidx[b, 0]], u[oidx[b, 1]]], axis=1)
-        return fold(dot_nt(x, w[b]))
-
-    GROUP = 6
+        x = jnp.concatenate([u[b], u[oidx[0, b]], u[oidx[1, b]]], axis=1)
+        return fold(dot_nn(x, w[b]))
+
+    GROUP = 15
+    BATCH = 5
 
     def middle(u, emit):
         def body(q, carry):
-            rows = [1 + q * GROUP + p for p in range(GROUP)]
-            ys = [row(u, b) for b in rows]
-            emit(rows, ys)
+            for first in range(0, GROUP, BATCH):
+                rows = [1 + q * GROUP + first + p for p in range(BATCH)]
+                emit(rows, [row(u, b) for b in rows])
             return carry
 
-        lax.fori_loop(0, (nb - 2) // GROUP, body, 0)
+        if GROUP == nb - 2:
+            body(0, 0)
+        else:
+            lax.fori_loop(0, (nb - 2) // GROUP, body, 0)
 
     def first_last(u):
-        y0 = row(u, 0) + fold(dot_nt(u[left], wc[0]))
-        y1 = row(u, nb - 1) + fold(dot_nt(u[right], wc[1]))
+        y0 = row(u, 0) + fold(dot_nn(u[left], wc[0]))
+        y1 = row(u, nb - 1) + fold(dot_nn(u[right], wc[1]))
         return y0, y1
 
     def outer(u):
-        yl = fold(dot_nt(jnp.concatenate([u[left], u[0]], axis=1), wt[0]))
-        yr = fold(dot_nt(jnp.concatenate([u[right], u[nb - 1]], axis=1), wt[1]))
+        yl = fold(dot_nn(jnp.concatenate([u[left], u[0]], axis=1), wt[0]))
+        yr = fold(dot_nn(jnp.concatenate([u[right], u[nb - 1]], axis=1), wt[1]))
         return yl, yr
 
     coefs = cheb_coefs()
@@ -394,16 +398,16 @@
 
     def init_w(b, carry):
         for j, v in enumerate((f_diag[b], f_offs[b, 0], f_offs[b, 1])):
-            hi, lo = halves(v)
-            w[b, 0:bs, j * bs : (j + 1) * bs] = hi
-            w[b, bs : 2 * bs, j * bs : (j + 1) * bs] = lo
+            hi, lo = halves(v.T)
+            w[b, j * bs : (j + 1) * bs, 0:bs] = hi
+            w[b, j * bs : (j + 1) * bs, bs : 2 * bs] = lo
         return carry
 
     lax.fori_loop(0, nb, init_w, 0)
     for j in range(2):
-        hi, lo = halves(f_couple[j])
-        wc[j, 0:bs, :] = hi
-        wc[j, bs : 2 * bs, :] = lo
+        hi, lo = halves(f_couple[j].T)
+        wc[j, :, 0:bs] = hi
+        wc[j, :, bs : 2 * bs] = lo
     ld[5].wait()
     for j in range(ncb):
         hi, lo = halves(f_cblk[j])
@@ -412,9 +416,9 @@
     wait_both(op_copies)
     for side in range(2):
         for j in range(2):
-            hi, lo = halves(op_in[side, j])
-            wt[side, 0:bs, j * bs : (j + 1) * bs] = hi
-            wt[side, bs : 2 * bs, j * bs : (j + 1) * bs] = lo
+            hi, lo = halves(op_in[side, j].T)
+            wt[side, j * bs : (j + 1) * bs, 0:bs] = hi
+            wt[side, j * bs : (j + 1) * bs, bs : 2 * bs] = lo
 
     for it in range(ITERS):
         iteration(it)
@@ -444,8 +448,8 @@
             pltpu.VMEM((2, bs, bs), F32),
             pltpu.VMEM((k * nb, bs), F32),
             pltpu.VMEM((ncb, bs, bs), F32),
-            pltpu.VMEM((nb, 2 * bs, 3 * bs), BF16),
-            pltpu.VMEM((2, 2 * bs, bs), BF16),
+            pltpu.VMEM((nb, 3 * bs, 2 * bs), BF16),
+            pltpu.VMEM((2, bs, 2 * bs), BF16),
             pltpu.VMEM((2, 2 * bs, 2 * bs), BF16),
             pltpu.VMEM((nb // 2, 2 * bs, 2 * bs), BF16),
             pltpu.VMEM((2 * bs, ncb * bs), BF16),
@@ -479,7 +483,7 @@
             collective_id=0, has_side_effects=True, vmem_limit_bytes=56 * 1024 * 1024
         ),
     )(
-        loads.reshape(cols * nb, bs), diag[0], offs[0], oidx[0], couple[0],
+        loads.reshape(cols * nb, bs), diag[0], offs[0], oidx[0].T, couple[0],
         basis.reshape(k * nb, bs), cblk[0], cidx[0],
     )
     return sol.transpose(1, 0, 2)[None], res.transpose(1, 0, 2)[None]

time: 59.6 us -> 49.3 us (0.83)
  Pallas kernels: 53 us -> 44.2 us
  local copies, waits for them, and re-layouts: 5.65 us -> 4.28 us
    pallas_call x1, Pallas kernels: 53 us -> 44.2 us  [per_device(): pl.pallas_call(functools.partial(kernel, ns, nc, nb, cols, bs, ncb), out_...]
    squeeze x1 -> x0, local copies, waits for them, and re-layouts: 1.36 us -> none  [per_device(): oidx[0]]
where the time goes in v2:
time: 49.3 us; the launch traced here: 49.1 us
  Pallas kernels  44.2 us (90%)
  local copies, waits for them, and re-layouts  4.28 us (9%)
  between operations  0.64 us (1%)
    pallas_call x1, Pallas kernels, per_device(): pl.pallas_call(functools.partial(kernel, ns, nc, nb, cols, bs, ncb), out_...  44.2 us
    unnamed x2, local copies, waits for them, and re-layouts  4.28 us

profile of v2, /device:TPU:1, one launch (start us, length us, event | category | flops | bytes accessed | tf_op | source)
XLA Modules:
  0.0 49.1 jit_solution(4169859131165664947)
XLA Ops:
  0.6 44.2 %shard_map.95 = (f32[32,32,128]{2,1,0:T(8,128)}, f32[32,32,128]{2,1,0:T(8,128)}) custom-call(f32[1024,128]{1,0:T(8,128)} %bitcast.19, f32[32,128,128]{2,1,0:T(8,128)} %bitcast.17, f32[32,2,128,128]{3,2,1,0:T(8,128)} %bitcast.16, s32[2,32]{1,0:T(2,128)} %bitcast.24, f32[2,128,128]{2,1,0:T(8,128)} %bitcast.23, f32[4096,128]{1,0:T(8,128)} %bitcast.18, ...), custom_call_target="tpu_custom_call" | custom-call | tf_op jit(solution)/shard_map/pallas_call | solution.py:439
  44.8 2.1 %copy.10 = f32[1,32,32,128]{3,2,1,0:T(8,128)} copy(f32[1,32,32,128]{3,1,2,0:T(8,128)} %bitcast.21) | data formatting | bytes 1048576
  47.0 2.1 %copy.11 = f32[1,32,32,128]{3,2,1,0:T(8,128)} copy(f32[1,32,32,128]{3,1,2,0:T(8,128)} %bitcast.20) | data formatting | bytes 1048576

commit v3 on v2

--- a/solution.py
+++ b/solution.py
@@ -9,6 +9,7 @@
 
 ORDER = 5
 ITERS = 2
+PARTS = 2
 THETA = 5.0
 DELTA = 4.0
 F32 = jnp.float32
@@ -195,31 +196,35 @@
     own = me_x * half + h
     gath = (gath0, gath1)
 
-    def g1(it):
+    def part(p):
+        return pl.ds(p * (cols // PARTS), cols // PARTS)
+
+    def g1(it, p):
         return [
             remote(
-                gath[it].at[core, own], gath[it].at[core, own],
-                g1_s.at[it, k - 1], g1_r.at[it, k - 1],
+                gath[it].at[core, own, part(p)], gath[it].at[core, own, part(p)],
+                g1_s.at[it * PARTS + p, k - 1], g1_r.at[it * PARTS + p, k - 1],
                 core + 2 * lax.rem(h + k, half), me_x,
             )
             for k in range(1, half)
         ]
 
-    def g2(it):
+    def g2(it, p):
         span = pl.ds(me_x * half, half)
         return [
             remote(
-                gath[it].at[core, span], gath[it].at[core, span],
-                g2_s.at[it, k - 1], g2_r.at[it, k - 1],
+                gath[it].at[core, span, part(p)], gath[it].at[core, span, part(p)],
+                g2_s.at[it * PARTS + p, k - 1], g2_r.at[it * PARTS + p, k - 1],
                 me_s, lax.rem(me_x + k, nc),
             )
             for k in range(1, nc)
         ]
 
-    def g3(it):
+    def g3(it, p):
         return [
             remote(
-                gath[it].at[core], gath[it].at[core], g3_s.at[it], g3_r.at[it], partner, me_x
+                gath[it].at[core, :, part(p)], gath[it].at[core, :, part(p)],
+                g3_s.at[it * PARTS + p], g3_r.at[it * PARTS + p], partner, me_x,
             )
         ]
 
@@ -311,17 +316,22 @@
             r[b] = v
             put(ur, b, v)
         ends_step(0, ur, ua)
-        wait(g1(it))
-        start(g2(it))
+        wait(g1(it, 0))
+        start(g2(it, 0))
         middle(ua, emit_step(1, ub))
         ends_step(1, ua, ub)
+        wait(g1(it, 1))
+        start(g2(it, 1))
         middle(ub, emit_step(2, ua))
         ends_step(2, ub, ua)
-        wait(g2(it))
-        start(g3(it))
+        wait(g2(it, 0))
+        start(g3(it, 0))
         ends_step(3, ua, ub)
         middle(ua, emit_step(3, ub))
-        wait(g3(it))
+        wait(g2(it, 1))
+        start(g3(it, 1))
+        wait(g3(it, 0))
+        wait(g3(it, 1))
 
         xs = []
         for j in range(ncb):
@@ -386,11 +396,13 @@
         middle(ub, emit_res)
         if not last:
             coeffs(it + 1)
-            start(g1(it + 1))
+            start(g1(it + 1, 0))
+            start(g1(it + 1, 1))
 
     start_both(functools.partial(r_copy, 0))
     coeffs(0)
-    start(g1(0))
+    start(g1(0, 0))
+    start(g1(0, 1))
     ld[2].wait()
     ld[3].wait()
     start_both(op_copies)
@@ -472,12 +484,12 @@
             dma((ITERS, 2)),
             dma((ITERS, 2)),
             dma((ITERS, 2)),
-            dma((ITERS, half - 1)),
-            dma((ITERS, half - 1)),
-            dma((ITERS, nc - 1)),
-            dma((ITERS, nc - 1)),
-            dma((ITERS,)),
-            dma((ITERS,)),
+            dma((ITERS * PARTS, half - 1)),
+            dma((ITERS * PARTS, half - 1)),
+            dma((ITERS * PARTS, nc - 1)),
+            dma((ITERS * PARTS, nc - 1)),
+            dma((ITERS * PARTS,)),
+            dma((ITERS * PARTS,)),
         ],
         compiler_params=pltpu.CompilerParams(
             collective_id=0, has_side_effects=True, vmem_limit_bytes=56 * 1024 * 1024

time: 49.3 us -> 49.3 us (level)
  no operation moved by 1% of the time
where the time goes in v3:
time: 49.3 us; the launch traced here: 49.1 us
  Pallas kernels  44.2 us (90%)
  local copies, waits for them, and re-layouts  4.28 us (9%)
  between operations  0.64 us (1%)
    pallas_call x1, Pallas kernels, per_device(): pl.pallas_call(functools.partial(kernel, ns, nc, nb, cols, bs, ncb), out_...  44.2 us
    unnamed x2, local copies, waits for them, and re-layouts  4.28 us

profile of v3, /device:TPU:1, one launch (start us, length us, event | category | flops | bytes accessed | tf_op | source)
XLA Modules:
  0.0 49.1 jit_solution(2738979877174709735)
XLA Ops:
  0.6 44.2 %shard_map.95 = (f32[32,32,128]{2,1,0:T(8,128)}, f32[32,32,128]{2,1,0:T(8,128)}) custom-call(f32[1024,128]{1,0:T(8,128)} %bitcast.19, f32[32,128,128]{2,1,0:T(8,128)} %bitcast.17, f32[32,2,128,128]{3,2,1,0:T(8,128)} %bitcast.16, s32[2,32]{1,0:T(2,128)} %bitcast.24, f32[2,128,128]{2,1,0:T(8,128)} %bitcast.23, f32[4096,128]{1,0:T(8,128)} %bitcast.18, ...), custom_call_target="tpu_custom_call" | custom-call | tf_op jit(solution)/shard_map/pallas_call | solution.py:451
  44.8 2.1 %copy.10 = f32[1,32,32,128]{3,2,1,0:T(8,128)} copy(f32[1,32,32,128]{3,1,2,0:T(8,128)} %bitcast.21) | data formatting | bytes 1048576
  46.9 2.1 %copy.11 = f32[1,32,32,128]{3,2,1,0:T(8,128)} copy(f32[1,32,32,128]{3,1,2,0:T(8,128)} %bitcast.20) | data formatting | bytes 1048576

commit v4 on v2

--- a/solution.py
+++ b/solution.py
@@ -116,18 +116,6 @@
         return carry
 
     lax.fori_loop(0, nb, init_r, 0)
-    ld[1].wait()
-
-    def init_bw(t, carry):
-        for p in range(2):
-            v = f_basis[pl.ds(2 * t + p, bs, stride=nb), :]
-            hi, lo = halves(v)
-            bw[t, 0:bs, p * bs : (p + 1) * bs] = hi
-            bw[t, bs : 2 * bs, p * bs : (p + 1) * bs] = lo
-        return carry
-
-    lax.fori_loop(0, nb2, init_bw, 0)
-
     pl.semaphore_wait(barrier, half - 1 + nc - 1 + has_l.astype(jnp.int32) + has_r.astype(jnp.int32))
 
     def op_copies(to_left):
@@ -135,9 +123,9 @@
         side = 1 if to_left else 0
         s = me_s - 1 if to_left else me_s + 1
         return [
-            remote(f_diag.at[b], op_in.at[side, 0], op_s.at[side, 0], op_r.at[side, 0], s, me_x),
+            remote(diag.at[b], op_in.at[side, 0], op_s.at[side, 0], op_r.at[side, 0], s, me_x),
             remote(
-                f_couple.at[0 if to_left else 1], op_in.at[side, 1],
+                couple.at[0 if to_left else 1], op_in.at[side, 1],
                 op_s.at[side, 1], op_r.at[side, 1], s, me_x,
             ),
         ]
@@ -191,6 +179,19 @@
             for it in range(ITERS):
                 r_in[it, side] = jnp.zeros_like(r_in[it, side])
                 e_in[it, side] = jnp.zeros_like(e_in[it, side])
+
+    start_both(op_copies)
+    ld[1].wait()
+
+    def init_bw(t, carry):
+        for p in range(2):
+            v = f_basis[pl.ds(2 * t + p, bs, stride=nb), :]
+            hi, lo = halves(v)
+            bw[t, 0:bs, p * bs : (p + 1) * bs] = hi
+            bw[t, bs : 2 * bs, p * bs : (p + 1) * bs] = lo
+        return carry
+
+    lax.fori_loop(0, nb2, init_bw, 0)
 
     own = me_x * half + h
     gath = (gath0, gath1)
@@ -302,9 +303,19 @@
         y0, y1 = first_last(u)
         emit_step(k, unew)([0, nb - 1, left, right], [y0, y1, yl, yr])
 
+    def outer_operator():
+        wait_both(op_copies)
+        for side in range(2):
+            for j in range(2):
+                hi, lo = halves(op_in[side, j].T)
+                wt[side, j * bs : (j + 1) * bs, 0:bs] = hi
+                wt[side, j * bs : (j + 1) * bs, bs : 2 * bs] = lo
+
     def iteration(it):
         last = it + 1 == ITERS
         middle(ur, emit_step(0, ua))
+        if it == 0:
+            outer_operator()
         wait_both(functools.partial(r_copy, it))
         for side, b in ((0, left), (1, right)):
             v = r_in[it, side]
@@ -393,7 +404,6 @@
     start(g1(0))
     ld[2].wait()
     ld[3].wait()
-    start_both(op_copies)
     ld[4].wait()
 
     def init_w(b, carry):
@@ -413,13 +423,6 @@
         hi, lo = halves(f_cblk[j])
         cw[0:bs, j * bs : (j + 1) * bs] = hi
         cw[bs : 2 * bs, j * bs : (j + 1) * bs] = lo
-    wait_both(op_copies)
-    for side in range(2):
-        for j in range(2):
-            hi, lo = halves(op_in[side, j].T)
-            wt[side, j * bs : (j + 1) * bs, 0:bs] = hi
-            wt[side, j * bs : (j + 1) * bs, bs : 2 * bs] = lo
-
     for it in range(ITERS):
         iteration(it)
 

time: 49.3 us -> 47.9 us (0.972)
  Pallas kernels: 44.2 us -> 42.7 us
    pallas_call x1, Pallas kernels: 44.2 us -> 42.7 us  [per_device(): pl.pallas_call(functools.partial(kernel, ns, nc, nb, cols, bs, ncb), out_...]
where the time goes in v4:
time: 47.9 us; the launch traced here: 47.6 us
  Pallas kernels  42.7 us (89%)
  local copies, waits for them, and re-layouts  4.28 us (9%)
  between operations  0.64 us (1%)
    pallas_call x1, Pallas kernels, per_device(): pl.pallas_call(functools.partial(kernel, ns, nc, nb, cols, bs, ncb), out_...  42.7 us
    unnamed x2, local copies, waits for them, and re-layouts  4.28 us

profile of v4, /device:TPU:1, one launch (start us, length us, event | category | flops | bytes accessed | tf_op | source)
XLA Modules:
  0.0 47.6 jit_solution(11859883527816300394)
XLA Ops:
  0.6 42.7 %shard_map.95 = (f32[32,32,128]{2,1,0:T(8,128)}, f32[32,32,128]{2,1,0:T(8,128)}) custom-call(f32[1024,128]{1,0:T(8,128)} %bitcast.19, f32[32,128,128]{2,1,0:T(8,128)} %bitcast.17, f32[32,2,128,128]{3,2,1,0:T(8,128)} %bitcast.16, s32[2,32]{1,0:T(2,128)} %bitcast.24, f32[2,128,128]{2,1,0:T(8,128)} %bitcast.23, f32[4096,128]{1,0:T(8,128)} %bitcast.18, ...), custom_call_target="tpu_custom_call" | custom-call | tf_op jit(solution)/shard_map/pallas_call | solution.py:442
  43.4 2.1 %copy.10 = f32[1,32,32,128]{3,2,1,0:T(8,128)} copy(f32[1,32,32,128]{3,1,2,0:T(8,128)} %bitcast.21) | data formatting | bytes 1048576
  45.5 2.1 %copy.11 = f32[1,32,32,128]{3,2,1,0:T(8,128)} copy(f32[1,32,32,128]{3,1,2,0:T(8,128)} %bitcast.20) | data formatting | bytes 1048576
